TPU v7x, 32 devices: a whole 2x2x4 slice. The times are simulated.
32 devices in a mesh: group: 2 (over y), sky: 4 (over z), visit: 2 (over x), band: 2 (over core).
Axes of the slice: x: 2, y: 2, z: 4, core: 2. Of those that a mesh axis runs over, the one named last changes fastest.
Arguments:
- raw_tiles: bfloat16 [16, 32, 128, 128], P(('group', 'visit', 'band'), 'sky'), parts along dimension 0, may hold values from -6 to 6
- pixel_offsets: int32 [16, 32, 2], P(('group', 'visit', 'band'), 'sky'), parts along dimension 0, may hold values from -1 to 1
- shift_entry_index: int32 [16, 32], P(('group', 'visit', 'band'), 'sky'), parts along dimension 0, may hold values from 0 to 15
- shift_table: float32 [16, 2], replicated, may hold values from 0 to 1
- tile_routes: int32 [16, 32], P(('group', 'visit', 'band'), 'sky'), parts along dimension 0, may hold values from 0 to 31, as said below
- bad_pixels: int32 [16, 32, 32], P('group', 'sky'), parts along dimension 0, may hold values from 0 to 16383, as said below
- basis_kernels: bfloat16 [4, 33, 33], replicated, may hold values from -0.5 to 0.5
- basis_choice: int32 [16, 32], P(('group', 'visit', 'band'), 'sky'), parts along dimension 0, may hold values from 0 to 15
- coef_table: float32 [16, 4], replicated, may hold values from -4 to 4
Outputs:
- difference: bfloat16 [16, 512, 1024], P(('group', 'visit', 'band'), 'sky'), parts along dimension 0
There are 2 independent parts, one for each index of `group`. A program takes and returns all parts, laid end to end along the dimension named above; an argument that names none is the same for every part. Nothing has to cross between parts.
Inputs may be any that keep to these rules, and one draw needn't show every extreme that they name: `tile_routes`: for every visit, each of the 32 slab tiles is named by exactly one source tile. Within each aligned block of 2 visits, the source tiles i with one value of i // 8 name at most 5 slab tiles t with one value of t // 8, and exactly 5 for some value. `bad_pixels`: an entry names the pixel at row r and column c of the slab tile as r * 128 + c. For one slab tile, the entries of all visits together are distinct.
All inputs are finite; a program needn't handle non-finite values.
Results may differ from a plain program's by a relative error of at most 0.018.
Values may be sent and summed in bfloat16 or wider, within the bound.
No kernel may reach another device: no remote copies, remote signals or barrier semaphores. Data moves between devices by JAX's collectives and lax.ppermute only.
A program may use at most 128 MiB of HBM per device.

v0:
```python
import jax
import jax.numpy as jnp
from jax import lax
from jax.sharding import PartitionSpec as P


def with_halo(block, sides, width):
    for axis, dim in sides:
        count = lax.axis_size(axis)
        forward = [(i, i + 1) for i in range(count - 1)]
        backward = [(target, source) for source, target in forward]
        low = lax.ppermute(
            lax.slice_in_dim(block, block.shape[dim] - width, None, axis=dim), axis, forward
        )
        high = lax.ppermute(lax.slice_in_dim(block, 0, width, axis=dim), axis, backward)
        block = jnp.concatenate([low, block, high], axis=dim)
    return block


def lanczos(offset):
    return jnp.where(jnp.abs(offset) < 3.0, jnp.sinc(offset) * jnp.sinc(offset / 3.0), 0.0)


def tiles_to_image(tiles):
    visit_count, tile_cols, tile_side = (tiles.shape[0], tiles.shape[1], tiles.shape[2])
    return jnp.transpose(tiles, (0, 2, 1, 3)).reshape(visit_count, tile_side, tile_cols * tile_side)


def hit_planes(listed, tile_side):
    indices = jnp.arange(tile_side)
    row_match_count = (listed[..., None, :] // tile_side == indices[:, None]).astype(jnp.bfloat16)
    column_match_count = (listed[..., None, :] % tile_side == indices[:, None]).astype(jnp.bfloat16)
    return jnp.einsum(
        "...am,...bm->...ab",
        row_match_count,
        column_match_count,
        preferred_element_type=jnp.float32,
    )


def warp_tiles(raw_tiles, pixel_offsets, shift_entry_index, shift_table):
    entries = shift_table.shape[0]
    tile_side = raw_tiles.shape[-1]
    selected_entries = (shift_entry_index[..., None] == jnp.arange(entries)).astype(jnp.float32)
    fraction = jnp.sum(selected_entries[..., None] * shift_table, axis=-2)
    shifts = pixel_offsets.astype(jnp.float32) + fraction
    target_positions = jnp.arange(tile_side).astype(jnp.float32)
    spacing = target_positions[:, None] - target_positions[None, :]
    row_weights = lanczos(spacing - shifts[..., 0, None, None]).astype(jnp.bfloat16)
    col_weights = lanczos(spacing - shifts[..., 1, None, None]).astype(jnp.bfloat16)
    halfway = jnp.einsum(
        "vtap,vtpq->vtaq", row_weights, raw_tiles, preferred_element_type=jnp.float32
    ).astype(jnp.bfloat16)
    return jnp.einsum(
        "vtaq,vtbq->vtab", halfway, col_weights, preferred_element_type=jnp.float32
    ).astype(jnp.bfloat16)


def banded_filter(padded, kernels, tile_side, tile_cols):
    kernel_side = kernels.shape[-1]
    window_width = tile_side + kernel_side - 1
    windows = jnp.stack(
        [padded[:, j * tile_side : j * tile_side + window_width] for j in range(tile_cols)]
    )
    offsets = jnp.arange(window_width)[:, None] - jnp.arange(tile_side)[None, :]
    inside = (offsets >= 0) & (offsets < kernel_side)
    bands = jnp.take(kernels, jnp.clip(offsets, 0, kernel_side - 1), axis=2)
    bands = jnp.where(inside[None, None], bands, jnp.zeros_like(bands))

    def one_tile(window):
        shifted = jnp.stack([window[dy : dy + tile_side] for dy in range(kernel_side)], axis=1)
        return jnp.einsum("adx,bdxc->bac", shifted, bands, preferred_element_type=jnp.float32)

    result = lax.map(one_tile, windows)
    basis_count = kernels.shape[0]
    return (
        jnp.transpose(result, (1, 2, 0, 3))
        .reshape(basis_count, tile_side, tile_cols * tile_side)
        .astype(jnp.bfloat16)
    )


def on_device(
    raw_tiles,
    pixel_offsets,
    shift_entry_index,
    shift_table,
    tile_routes,
    bad_pixels,
    basis_kernels,
    basis_choice,
    coef_table,
):
    visit_count, tile_cols, tile_side = (raw_tiles.shape[0], raw_tiles.shape[1], raw_tiles.shape[2])
    tile_area = tile_side * tile_side
    patches = lax.axis_size("sky")
    capacity = (visit_count * tile_cols + patches - 1) // patches + 1
    seat_count = patches * capacity
    warped = warp_tiles(raw_tiles, pixel_offsets, shift_entry_index, shift_table)
    owners = tile_routes // tile_cols
    slot_ids = tile_routes % tile_cols
    before = jnp.arange(tile_cols)[None, :] < jnp.arange(tile_cols)[:, None]
    shared = owners[:, None, :] == owners[:, :, None]
    queue_rank = jnp.sum(shared & before[None], axis=2)
    seat_ids = owners * capacity + queue_rank
    layout = seat_ids[:, None, :] == jnp.arange(seat_count)[None, :, None]
    outgoing = jnp.einsum(
        "vsk,vkx->vsx",
        layout.astype(jnp.bfloat16),
        warped.reshape(visit_count, tile_cols, tile_area),
        preferred_element_type=jnp.float32,
    ).astype(jnp.bfloat16)
    labels = (jnp.sum(jnp.where(layout, slot_ids[:, None, :] + 1, 0), axis=2) - 1).astype(
        jnp.bfloat16
    )
    arrived, arrived_labels = (
        lax.all_to_all(
            outgoing.reshape(visit_count, patches, capacity * tile_area),
            "sky",
            split_axis=1,
            concat_axis=1,
            tiled=True,
        ),
        lax.all_to_all(
            labels.reshape(visit_count, patches, capacity),
            "sky",
            split_axis=1,
            concat_axis=1,
            tiled=True,
        ),
    )
    landing = (
        arrived_labels.astype(jnp.float32).reshape(visit_count, seat_count)[:, None, :]
        == jnp.arange(tile_cols).astype(jnp.float32)[None, :, None]
    )
    placed = jnp.einsum(
        "vks,vsx->vkx",
        landing.astype(jnp.bfloat16),
        arrived.reshape(visit_count, seat_count, tile_area),
        preferred_element_type=jnp.float32,
    ).astype(jnp.bfloat16)
    slab_image = tiles_to_image(placed.reshape(visit_count, tile_cols, tile_side, tile_side))
    shard_index = lax.axis_index(("visit", "band"))
    visit_total = bad_pixels.shape[0]
    listed_count = bad_pixels.shape[2]
    own_listed = lax.dynamic_slice_in_dim(bad_pixels, shard_index * visit_count, visit_count, 0)
    own_flags = tiles_to_image(hit_planes(own_listed, tile_side))
    valid_pixel_mask = 1.0 - own_flags
    all_listed = jnp.transpose(bad_pixels, (1, 0, 2)).reshape(
        1, tile_cols, visit_total * listed_count
    )
    all_flags = tiles_to_image(hit_planes(all_listed, tile_side))[0]
    tallies = visit_total - all_flags
    values = slab_image.astype(jnp.float32)
    partial_sums = jnp.sum(valid_pixel_mask * values, axis=0)
    partial_high = jnp.max(jnp.where(valid_pixel_mask > 0.5, slab_image, -jnp.inf), axis=0)
    partial_low = jnp.min(jnp.where(valid_pixel_mask > 0.5, slab_image, jnp.inf), axis=0)
    summed = lax.psum(partial_sums.astype(jnp.bfloat16), ("visit", "band")).astype(jnp.float32)
    highest = lax.pmax(partial_high, ("visit", "band"))
    lowest = lax.pmin(partial_low, ("visit", "band"))
    coadded = (
        (summed - highest.astype(jnp.float32) - lowest.astype(jnp.float32)) / (tallies - 2.0)
    ).astype(jnp.bfloat16)
    margin = basis_kernels.shape[-1] // 2
    padded = with_halo(coadded, (("sky", 0),), margin)
    padded = jnp.pad(padded, ((0, 0), (margin, margin)))
    per_device = basis_kernels.shape[0] // lax.axis_size("visit")
    own_kernels = lax.dynamic_slice_in_dim(
        basis_kernels, lax.axis_index("visit") * per_device, per_device, 0
    )
    filtered = lax.all_gather(
        banded_filter(padded, own_kernels, tile_side, tile_cols), "visit", axis=0, tiled=True
    )
    entries = coef_table.shape[0]
    picks = (basis_choice[..., None] == jnp.arange(entries)).astype(jnp.float32)
    mixture = jnp.sum(picks[..., None] * coef_table, axis=2)
    basis_count = basis_kernels.shape[0]
    basis_planes = filtered.astype(jnp.float32).reshape(
        basis_count, tile_side, tile_cols, tile_side
    )
    template = jnp.einsum(
        "vkb,bakc->vakc", mixture, basis_planes, precision=lax.Precision.HIGHEST
    ).reshape(visit_count, tile_side, tile_cols * tile_side)
    return ((values - template) * valid_pixel_mask).astype(jnp.bfloat16)


def solution(mesh):
    return jax.shard_map(
        on_device,
        mesh=mesh,
        in_specs=(
            P(("group", "visit", "band"), "sky", None, None),
            P(("group", "visit", "band"), "sky", None),
            P(("group", "visit", "band"), "sky"),
            P(),
            P(("group", "visit", "band"), "sky"),
            P("group", "sky", None),
            P(),
            P(("group", "visit", "band"), "sky"),
            P(),
        ),
        out_specs=P(("group", "visit", "band"), "sky", None),
        check_vma=False,
    )
```

profile of v0, /device:TPU:0, one launch (start us, length us, event | category | flops | bytes accessed | tf_op | source)
XLA Modules:
  0.0 321.6 jit_solution(13471910060581517322)
XLA Ops:
  6.5 0.7 fusion.170
  7.7 0.6 copy.60
  8.3 6.3 %all-to-all-start = ((bf16[2,4,5]{2,0,1:T(2,128)(2,1)}), bf16[2,4,5]{2,0,1:T(2,128)(2,1)S(1)}, u32[]{:S(2)}, u32[]{:S(2)}) async-start(bf16[2,4,5]{2,0,1:T(2,128)(2,1)} %copy.60), calls=%async_computation | async-start | bytes 4096 | tf_op jit(solution)/shard_map/all_to_all | solution.py:124
  14.6 0.7 fusion.161
  15.4 0.8 multiply_reduce_fusion.1
  16.2 0.7 convert_add_fusion
  16.9 5.2 %convolution_convert_fusion.2 = bf16[2,8,128,128]{3,2,1,0:T(8,128)(2,1)S(1)} fusion(bf16[2,8,128,128]{3,2,1,0:T(8,128)(2,1)S(1)} %copy-done, f32[2,8]{1,0:T(2,128)S(1)} %bitcast.308, f32[2,8]{1,0:T(2,128)S(1)} %bitcast.307, f32[128,128]{1,0:T(8,128)S(1)} %broadcast_subtract_fusion), kind=kOutput, calls=%fused_computation.124 | convolution fusion | flops 172490752 | bytes 1114240 | tf_op jit(solution)/shard_map/vtaq,vtbq->vtab/dot_general | solution.py:54
  22.4 0.7 convolution_convert_fusion
  23.0 1.6 reshape.362
  24.6 2.4 copy.62
  27.0 5.2 %all-to-all-start.1 = ((bf16[2,4,81920]{2,0,1:T(2,128)(2,1)}), bf16[2,4,81920]{2,0,1:T(2,128)(2,1)S(1)}, u32[]{:S(2)}, u32[]{:S(2)}) async-start(bf16[2,4,81920]{2,0,1:T(2,128)(2,1)} %copy.62), calls=%async_computation.1 | async-start | bytes 2621440 | tf_op jit(solution)/shard_map/all_to_all | solution.py:117
  32.5 30.5 %all-to-all-done.1 = bf16[2,4,81920]{2,0,1:T(2,128)(2,1)S(1)} async-done(((bf16[2,4,81920]{2,0,1:T(2,128)(2,1)}), bf16[2,4,81920]{2,0,1:T(2,128)(2,1)S(1)}, u32[]{:S(2)}, u32[]{:S(2)}) %all-to-all-start.1) | async-done | bytes 1310752 | tf_op jit(solution)/shard_map/all_to_all | solution.py:117
  63.0 1.0 copy.63
  64.0 0.9 reshape.363
  65.0 0.4 fusion.32
  65.4 0.4 copy.64
  65.8 1.9 fusion.106
  67.7 1.0 copy-done.3
  68.6 0.8 fusion.33
  69.6 0.7 all-reduce.7.cloned.1.call-update
  70.3 1.2 convolution_subtract_fusion.1
  71.8 132.1 %gather_fusion = bf16[20480,2,33]{2,1,0:T(2,128)(2,1)} fusion(bf16[2,33,33]{1,0,2:T(2,128)(2,1)S(1)} %copy.83, s32[20480]{0:T(1024)S(1)} %fusion.144), kind=kCustom, calls=%fused_computation | custom fusion | bytes 5488640 | tf_op jit(solution)/shard_map/jit(_take)/gather | solution.py:67
  203.9 15.1 %copy.78 = bf16[160,128,2,33]{1,0,2,3:T(8,128)(2,1)S(1)} copy(bf16[160,128,2,33]{3,2,1,0:T(2,128)(2,1)} %bitcast.298) | data formatting | bytes 5406720 | tf_op jit(solution)/shard_map/jit(_take)/gather | solution.py:67
  219.2 1.4 fusion.105
  220.6 0.9 fusion.197
  221.4 2.0 collective-permute-start
  223.4 1.3 collective-permute-start.1
  224.7 1.8 select_bitcast_fusion
  226.6 3.5 %copy.68 = bf16[2,33,160,128]{3,2,1,0:T(8,128)(2,1)} copy(bf16[2,33,160,128]{3,2,0,1:T(8,128)(2,1)} %select_bitcast_fusion) | data formatting | bytes 5406720 | tf_op jit(solution)/shard_map/while | solution.py:74
  230.1 2.9 collective-permute-done.1
  233.0 1.3 pad_maximum_fusion
  234.4 48.8 %while.10 = (s32[]{:T(128)}, bf16[8,2,128,128]{2,3,0,1:T(8,128)(2,1)S(1)}, bf16[8,160,160]{1,2,0:T(8,128)(2,1)S(1)}, bf16[2,33,160,128]{3,2,1,0:T(8,128)(2,1)}, ...) while((s32[]{:T(128)}, ...), condition=%wide.region_10.12_spmd, body=%wide.region_9.11_spmd.sunk | while | flops 346030112 | bytes 7087053 | solution.py:74
  238.0 2.4 fusion.211
  244.0 2.4 fusion.211
  250.1 2.4 fusion.211
  256.2 2.4 fusion.211
  262.3 2.4 fusion.211
  268.4 2.4 fusion.211
  274.5 2.4 fusion.211
  280.6 2.4 fusion.211
  283.2 1.0 copy.70
  284.5 20.7 %all-gather.2.cloned.1.call-done = bf16[4,128,1024]{2,1,0:T(8,128)(2,1)} async-done(((bf16[2,128,1024]{2,1,0:T(8,128)(2,1)}), bf16[4,128,1024]{2,1,0:T(8,128)(2,1)}) %all-gather.2.cloned.1.call-update) | async-done | bytes 1048592 | tf_op jit(solution)/shard_map/all_gather | solution.py:171
  305.2 1.6 copy.71
  306.8 0.7 copy.72
  307.6 2.8 fusion.199
  310.3 1.6 copy.74
  312.0 1.0 fusion.35
  313.0 2.0 copy.75
  (343 shorter events, 30.2 us)
Async XLA Ops:
  6.5 10.4 %copy-start = (bf16[2,8,128,128]{3,2,1,0:T(8,128)(2,1)S(1)}, bf16[2,8,128,128]{3,2,1,0:T(8,128)(2,1)}, u32[]{:S(2)}) copy-start(bf16[2,8,128,128]{3,2,1,0:T(8,128)(2,1)} %param.12) | copy-start | bytes 1572868
  8.3 18.7 %all-to-all-start = ((bf16[2,4,5]{2,0,1:T(2,128)(2,1)}), bf16[2,4,5]{2,0,1:T(2,128)(2,1)S(1)}, u32[]{:S(2)}, u32[]{:S(2)}) async-start(bf16[2,4,5]{2,0,1:T(2,128)(2,1)} %copy.60), calls=%async_computation | async-start | bytes 4096 | tf_op jit(solution)/shard_map/all_to_all | solution.py:124
  27.0 5.2 %copy-start.5 = (s32[8,8,32]{2,1,0:T(8,128)S(1)}, s32[8,8,32]{2,1,0:T(8,128)}, u32[]{:S(2)}) copy-start(s32[8,8,32]{2,1,0:T(8,128)} %param.17) | copy-start | bytes 24580
  27.0 36.0 %all-to-all-start.1 = ((bf16[2,4,81920]{2,0,1:T(2,128)(2,1)}), bf16[2,4,81920]{2,0,1:T(2,128)(2,1)S(1)}, u32[]{:S(2)}, u32[]{:S(2)}) async-start(bf16[2,4,81920]{2,0,1:T(2,128)(2,1)} %copy.62), calls=%async_computation.1 | async-start | bytes 2621440 | tf_op jit(solution)/shard_map/all_to_all | solution.py:117
  32.2 186.8 %all-reduce.5.cloned.1.call-start = ((), (), s32[]{:S(2)}) async-start(), calls=%async_computation.2 | async-start | bytes 524288 | tf_op jit(solution)/shard_map/psum | solution.py:158
  65.8 3.7 %copy-start.1 = (bf16[2,8,128,128]{2,3,1,0:T(8,128)(2,1)}, bf16[2,8,128,128]{2,3,1,0:T(8,128)(2,1)S(1)}, u32[]{:S(2)}) copy-start(bf16[2,8,128,128]{2,3,1,0:T(8,128)(2,1)S(1)} %copy.64) | copy-start | bytes 1572868
  67.7 1.0 copy-start.3
  69.5 2.1 copy-start.6
  69.5 149.6 %all-reduce.7.cloned.1.call-start = ((), (), s32[]{:S(2)}) async-start(), calls=%async_computation.3 | async-start | bytes 524288 | tf_op jit(solution)/shard_map/pmax | solution.py:159
  70.3 148.9 %all-reduce.9.cloned.1.call-start = ((), (), s32[]{:S(2)}) async-start(), calls=%async_computation.4 | async-start | bytes 524288 | tf_op jit(solution)/shard_map/pmin | solution.py:160
  71.6 233.6 %all-gather.2.cloned.1.call-start = ((), (), s32[]{:S(2)}) async-start(), calls=%async_computation.5 | async-start | bytes 1572864 | tf_op jit(solution)/shard_map/all_gather | solution.py:171
  221.4 8.6 %collective-permute-start = (bf16[16,1024]{0,1:T(8,128)(2,1)}, bf16[16,1024]{0,1:T(8,128)(2,1)}, u32[]{:S(2)}, u32[]{:S(2)}) collective-permute-start(bf16[16,1024]{0,1:T(8,128)(2,1)} %get-tuple-element.57), channel_id=1, source_target_pairs={{0,4},{4,8},{8,12},{1,5},{5,9},{9,13},{2,6},{6,10},{10,14},{3,7},{... | collective-permute-start | bytes 98312 | tf_op jit(solution)/shard_map/ppermute | solution.py:12
  223.4 9.5 %collective-permute-start.1 = (bf16[16,1024]{0,1:T(8,128)(2,1)}, bf16[16,1024]{0,1:T(8,128)(2,1)}, u32[]{:S(2)}, u32[]{:S(2)}) collective-permute-start(bf16[16,1024]{0,1:T(8,128)(2,1)} %get-tuple-element.58), channel_id=1, source_target_pairs={{4,0},{8,4},{12,8},{5,1},{9,5},{13,9},{6,2},{10,6},{14,10},{7,3},{... | collective-permute-start | bytes 98312 | tf_op jit(solution)/shard_map/ppermute | solution.py:15
  283.2 1.1 copy-start.8
  283.2 1.1 copy-start.7
  310.3 1.6 copy-start.2
  310.3 1.7 copy-start.4
Sparse Core Ops, SparseCore 0:
  69.6 31.3 all-reduce.4
  103.4 32.4 all-reduce.6
  138.2 32.4 all-reduce.8
  284.4 20.7 all-gather.1
where the time goes:
time: 323 us; the launch traced here: 322 us
  local copies, waits for them, and re-layouts  196 us (61%)
  waiting for transfers between devices  54.8 us (17%)
  matrix products  31.6 us (10%)
  starting transfers between devices  15 us (5%)
  between operations  13.5 us (4%)
  other arithmetic  10 us (3%)
    gather x2, local copies, waits for them, and re-layouts, banded_filter(): bands = jnp.take(kernels, jnp.clip(offsets, 0, kernel_side - 1), axis=2)  147 us
    all_to_all x1, waiting for transfers between devices, on_device(): lax.all_to_all(outgoing.reshape(visit_count, patches, capacity * tile_are...  30.5 us
    while x256, local copies, waits for them, and re-layouts  26.3 us
    all_gather x1, waiting for transfers between devices, on_device(): lax.all_gather(banded_filter(padded, own_kernels, tile_side, tile_cols),...  20.7 us
    dot_general x8, matrix products, one_tile(): jnp.einsum('adx,bdxc->bac', shifted, bands, preferred_element_type=jnp.fl...  19.5 us
  transfers between devices with their start and end apart: 8, of which 3 were waited for; matrix products, arithmetic and copies ran while one was open for 52% of the time, Pallas kernels for 0%

commit v1 on v0

v1 whole, which is shorter than its diff:
```python
import functools

import jax
import jax.numpy as jnp
from jax import lax
from jax.experimental import pallas as pl
from jax.experimental.pallas import tpu as pltpu
from jax.sharding import PartitionSpec as P

BF = jnp.bfloat16
F32 = jnp.float32
I32 = jnp.int32
VMEM = pl.BlockSpec(memory_space=pltpu.VMEM)
SMEM = pl.BlockSpec(memory_space=pltpu.SMEM)
LABELS = 8


def kernel_call(body, outs, in_specs, scratch=(), flops=0, data=0, name=None):
    return pl.pallas_call(
        body,
        out_shape=outs,
        in_specs=in_specs,
        out_specs=jax.tree.map(lambda _: VMEM, outs),
        scratch_shapes=list(scratch),
        cost_estimate=pl.CostEstimate(flops=flops, bytes_accessed=data, transcendentals=0),
        name=name,
    )


def sinc(x):
    angle = x * jnp.float32(jnp.pi)
    safe = jnp.where(x == 0.0, 1.0, angle)
    return jnp.where(x == 0.0, 1.0, jnp.sin(safe) / safe)


def iota(shape, dim):
    return lax.broadcasted_iota(I32, shape, dim)


def warp_body(patches, visits, cap, routes, offsets, entries, table, raw, *refs):
    parcels, (seats, labels, count) = refs[:-3], refs[-3:]
    visit_count, tile_cols, side, _ = raw.shape
    tiles = visit_count * tile_cols
    part = side // visits
    sky, visit = lax.axis_index("sky"), lax.axis_index("visit")
    row = iota((2 * tiles, side), 0)
    shift = jnp.zeros((2 * tiles, side), F32)
    for n in range(tiles):
        v, i = divmod(n, tile_cols)
        entry = entries[v, i]
        for axis in range(2):
            amount = offsets[v, i, axis].astype(F32) + table[entry, axis]
            shift = jnp.where(row == 2 * n + axis, amount, shift)
    lane = iota((2 * tiles, side), 1)
    step = jnp.where(lane < side // 2, lane, lane - side)
    x = jnp.where(row % 2 == 0, -step, step).astype(F32) - shift
    taps = jnp.where(jnp.abs(x) < 3.0, sinc(x) * sinc(x / 3.0), 0.0)
    near = jnp.abs(iota((side, side), 1) - iota((side, side), 0)) < side // 2

    def spread(index):
        rows = jnp.broadcast_to(taps[index : index + 1, :], (side, side))
        rolled = pltpu.roll(rows, 0, 1, stride=1, stride_axis=0)
        return jnp.where(near, rolled, 0.0).astype(BF)

    for k in range(patches):
        count[k] = 0
        labels[k] = jnp.full((LABELS, side), -1.0, F32)
    for n in range(tiles):
        v, i = divmod(n, tile_cols)
        halfway = jnp.dot(spread(2 * n), raw[v, i], preferred_element_type=F32).astype(BF)
        warped = jnp.dot(halfway, spread(2 * n + 1), preferred_element_type=F32).astype(BF)
        route = routes[v, i]
        owner = lax.div(route, tile_cols)
        slot = route - owner * tile_cols
        relative = lax.rem(owner - sky + patches, patches)
        seat = count[relative]
        count[relative] = seat + 1
        seats[relative * cap + seat] = warped
        labels[relative, pl.ds(seat, 1), :] = jnp.full(
            (1, side), ((visit * visit_count + v) * tile_cols + slot).astype(F32), F32
        )
    for k in range(patches):
        for r in range(visits):
            parcel = parcels[k * visits + r]
            target = lax.rem(visit + r, visits)
            rows = pl.ds(pl.multiple_of(target * part, part), part)
            for seat in range(cap):
                parcel[seat * part : (seat + 1) * part, :] = seats[k * cap + seat, rows, :]
            parcel[cap * part :, :] = labels[k].astype(BF)


def warp_tiles(patches, visits, cap, raw, offsets, entries, table, routes):
    visit_count, tile_cols, side, _ = raw.shape
    parcel = jax.ShapeDtypeStruct((cap * (side // visits) + LABELS, side), BF)
    return kernel_call(
        functools.partial(warp_body, patches, visits, cap),
        [parcel] * (patches * visits),
        [SMEM] * 4 + [VMEM],
        [
            pltpu.VMEM((patches * cap, side, side), BF),
            pltpu.VMEM((patches, LABELS, side), F32),
            pltpu.SMEM((patches,), I32),
        ],
        flops=4 * visit_count * tile_cols * side**3,
        data=4 * raw.size,
        name="warp",
    )(routes, offsets, entries, table, raw)


def tables_body(side, block, listed, taps, plane, bands):
    visit_total, tile_cols, per = listed.shape
    width = visit_total * per
    bad = jnp.concatenate([listed[v] for v in range(visit_total)], axis=1)
    bad_row = lax.div(bad, side)
    bad_col = bad - bad_row * side
    place = iota((side, width), 0)
    weight = (lax.div(iota((side, width), 1), per) + 1).astype(F32)
    for t in range(tile_cols):
        rows = jnp.where(bad_row[t : t + 1, :] == place, 1.0, 0.0).astype(BF)
        cols = jnp.where(bad_col[t : t + 1, :] == place, weight, 0.0).astype(BF)
        plane[:, t * side : (t + 1) * side] = lax.dot_general(
            rows, cols, (((1,), (1,)), ((), ())), preferred_element_type=F32
        )
    bases, pairs, lanes = taps.shape
    for b in range(bases):
        for j in range(pairs):
            rows = jnp.broadcast_to(taps[b, j : j + 1, :], (block, lanes))
            bands[b * block : (b + 1) * block, j * lanes : (j + 1) * lanes] = pltpu.roll(
                rows, 0, 1, stride=1, stride_axis=0
            ).astype(BF)


def make_tables(listed, kernels, side, block):
    visit_total, tile_cols, per = listed.shape
    bases, taps, _ = kernels.shape
    window = block + taps - 1
    group = max(1, 128 // window)
    padded = -(-taps // group) * group
    columns = jnp.pad(
        jnp.transpose(kernels, (0, 2, 1)).astype(F32), ((0, 0), (0, padded - taps), (0, window - taps))
    ).reshape(bases, padded // group, group * window)
    return kernel_call(
        functools.partial(tables_body, side, block),
        [
            jax.ShapeDtypeStruct((side, tile_cols * side), F32),
            jax.ShapeDtypeStruct((bases * block, padded * window), BF),
        ],
        [VMEM] * 2,
        flops=2 * tile_cols * side * side * visit_total * per,
        data=4 * side * side * tile_cols,
        name="tables",
    )(listed, columns)


def land_body(visits, bands, visit_count, cap, plane, *refs):
    count = len(refs) - 2 - visits
    parcels, slabs, partial, image = refs[:count], refs[count:-2], refs[-2], refs[-1]
    side = parcels[0].shape[1]
    part = (parcels[0].shape[0] - LABELS) // cap
    tile_cols = image.shape[2] // side
    held = visits * visit_count
    visit, band = lax.axis_index("visit"), lax.axis_index("band")
    for parcel in parcels:
        labels = parcel[cap * part :, :].astype(F32)
        for seat in range(cap):
            label = labels[seat, 0].astype(I32)
            label = jnp.where(label < 0, held * tile_cols, label)
            which = lax.div(label, tile_cols)
            column = (label - which * tile_cols) * side
            image[which, :, pl.ds(pl.multiple_of(column, side), side)] = parcel[
                seat * part : (seat + 1) * part, :
            ]
    mine = plane[pl.ds(pl.multiple_of(visit * part, part), part), :]
    total = jnp.zeros(mine.shape, F32)
    high = jnp.full(mine.shape, -jnp.inf, F32)
    low = jnp.full(mine.shape, jnp.inf, F32)
    for n in range(held):
        own, local = divmod(n, visit_count)
        number = ((own * bands + band) * visit_count + local + 1).astype(F32)
        value = image[n].astype(F32)
        bad = mine == number
        total = total + jnp.where(bad, 0.0, value)
        high = jnp.maximum(high, jnp.where(bad, -jnp.inf, value))
        low = jnp.minimum(low, jnp.where(bad, jnp.inf, value))
    partial[0] = total.astype(BF)
    partial[1] = high.astype(BF)
    partial[2] = low.astype(BF)
    for r in range(visits):
        base = lax.rem(visit + r, visits) * visit_count
        for j in range(visit_count):
            slabs[r][j] = image[base + j]


def land_tiles(visits, bands, visit_count, cap, tile_cols, plane, parcels):
    side = parcels[0].shape[1]
    part = (parcels[0].shape[0] - LABELS) // cap
    width = tile_cols * side
    out = kernel_call(
        functools.partial(land_body, visits, bands, visit_count, cap),
        [jax.ShapeDtypeStruct((visit_count, part, width), BF)] * visits
        + [jax.ShapeDtypeStruct((3, part, width), BF)],
        [VMEM] * (1 + len(parcels)),
        [pltpu.VMEM((visits * visit_count + 1, part, width), BF)],
        flops=10 * visits * visit_count * part * width,
        data=4 * visits * visit_count * part * width,
        name="land",
    )(plane, *parcels)
    return out[:-1], out[-1]


def coadd_body(visit_total, margin, plane, *refs):
    partials, (coadd, edge) = refs[:-2], refs[-2:]
    part = coadd.shape[0]
    visit = lax.axis_index("visit")
    mine = plane[pl.ds(pl.multiple_of(visit * part, part), part), :]
    total, high, low = (partials[0][n].astype(F32) for n in range(3))
    for other in partials[1:]:
        total = total + other[0].astype(F32)
        high = jnp.maximum(high, other[1].astype(F32))
        low = jnp.minimum(low, other[2].astype(F32))
    scale = jnp.where(mine > 0.0, 1.0 / (visit_total - 3.0), 1.0 / (visit_total - 2.0))
    coadd[...] = ((total - high - low) * scale).astype(BF)
    start = pl.multiple_of(jnp.where(visit == 0, 0, part - margin), margin)
    edge[...] = coadd[pl.ds(start, margin), :]


def filter_body(visits, margin, bands, *refs):
    pieces, halos = refs[:visits], refs[visits : 2 * visits]
    out, image, moved = refs[2 * visits :]
    visit = lax.axis_index("visit")
    part, width = pieces[0].shape
    taps = moved.shape[0]
    above, below = halos[0][...], halos[0][...]
    for r in range(visits):
        below = jnp.where(visit == r, halos[r][...], below)
        above = jnp.where(visits - 1 - visit == r, halos[r][...], above)
    image[:margin, :] = above.astype(F32)
    image[margin + visits * part :, :] = below.astype(F32)
    for r in range(visits):
        start = pl.multiple_of(lax.rem(visit + r, visits) * part + margin, margin)
        image[pl.ds(start, part), :] = pieces[r][...].astype(F32)
    column = iota((image.shape[0], width), 1)
    for dx in range(taps):
        rolled = pltpu.roll(image[...], (margin - dx) % width, 1)
        if dx < margin:
            rolled = jnp.where(column >= margin - dx, rolled, 0.0)
        elif dx > margin:
            rolled = jnp.where(column < width + margin - dx, rolled, 0.0)
        moved[dx] = rolled.astype(BF)
    blocks = out.shape[0]
    block = visits * part // blocks
    window = block + 2 * margin
    step = min(256, width)
    left = bands[:, : taps * window]
    for n in range(blocks):
        for c in range(0, width, step):
            right = moved[:, n * block : n * block + window, c : c + step].reshape(taps * window, step)
            out[n, :, c : c + step] = jnp.dot(left, right, preferred_element_type=F32).astype(BF)


def finish_body(visits, bands, choice, coefs, filtered, plane, *refs):
    slabs, out, image = refs[:visits], refs[-2], refs[-1]
    visit, band = lax.axis_index("visit"), lax.axis_index("band")
    visit_count, part, width = slabs[0].shape
    blocks = filtered.shape[0]
    bases = coefs.shape[1]
    block = filtered.shape[1] // bases
    tile_cols = choice.shape[1]
    side = width // tile_cols
    for r in range(visits):
        start = pl.multiple_of(lax.rem(visit + r, visits) * part, part)
        image[:, pl.ds(start, part), :] = slabs[r][...]
    for t in range(tile_cols):
        cols = slice(t * side, (t + 1) * side)
        mixture = [
            [coefs[choice[j, t], b] for b in range(bases)] for j in range(visit_count)
        ]
        for n in range(blocks):
            rows = slice(n * block, (n + 1) * block)
            planes = [
                filtered[n, b * block : (b + 1) * block, cols].astype(F32) for b in range(bases)
            ]
            bad = plane[rows, cols]
            for j in range(visit_count):
                template = sum(m * p for m, p in zip(mixture[j], planes))
                number = ((visit * bands + band) * visit_count + j + 1).astype(F32)
                value = image[j, rows, cols].astype(F32) - template
                out[j, rows, cols] = jnp.where(bad == number, 0.0, value).astype(BF)


def on_device(
    raw_tiles,
    pixel_offsets,
    shift_entry_index,
    shift_table,
    tile_routes,
    bad_pixels,
    basis_kernels,
    basis_choice,
    coef_table,
):
    visit_count, tile_cols, side = raw_tiles.shape[:3]
    patches, visits, bands = (lax.axis_size(name) for name in ("sky", "visit", "band"))
    cap = (visit_count * tile_cols + patches - 1) // patches + 1
    part, width = side // visits, tile_cols * side
    visit_total = bad_pixels.shape[0]
    bases, taps = basis_kernels.shape[:2]
    margin = taps // 2
    block = 2 * margin

    parcels = warp_tiles(
        patches, visits, cap, raw_tiles, pixel_offsets, shift_entry_index, shift_table, tile_routes
    )
    order = sorted(
        range(1, patches * visits), key=lambda n: -min(n // visits, patches - n // visits)
    )
    arrived = [parcels[0]]
    for n in order:
        k, r = divmod(n, visits)
        pairs = [
            (s * visits + v, (s + k) % patches * visits + (v + r) % visits)
            for s in range(patches)
            for v in range(visits)
        ]
        arrived.append(lax.ppermute(parcels[n], ("sky", "visit"), pairs))
    plane, toeplitz = make_tables(bad_pixels, basis_kernels, side, block)
    slabs, partial = land_tiles(visits, bands, visit_count, cap, tile_cols, plane, arrived)

    partials = [partial] + [
        lax.ppermute(partial, "band", [(b, (b + q) % bands) for b in range(bands)])
        for q in range(1, bands)
    ]
    coadd, edge = kernel_call(
        functools.partial(coadd_body, visit_total, margin),
        [jax.ShapeDtypeStruct((part, width), BF), jax.ShapeDtypeStruct((margin, width), BF)],
        [VMEM] * (1 + bands),
        flops=8 * part * width,
        data=8 * part * width,
        name="coadd",
    )(plane, *partials)

    def turn(r):
        return [(v, (v - r) % visits) for v in range(visits)]

    pieces = [coadd] + [lax.ppermute(coadd, "visit", turn(r)) for r in range(1, visits)]
    halos = []
    for r in range(visits):
        top = [(s * visits, (s - 1) * visits + r) for s in range(1, patches)]
        bottom = [
            (s * visits + visits - 1, (s + 1) * visits + visits - 1 - r) for s in range(patches - 1)
        ]
        halos.append(lax.ppermute(edge, ("sky", "visit"), top + bottom))
    own = [slabs[0]] + [
        lax.ppermute(slabs[r], "visit", [(v, (v + r) % visits) for v in range(visits)])
        for r in range(1, visits)
    ]
    own = [own[0]] + [own[visits - r] for r in range(1, visits)]
    filtered = kernel_call(
        functools.partial(filter_body, visits, margin),
        jax.ShapeDtypeStruct((side // block, bases * block, width), BF),
        [VMEM] * (1 + 2 * visits),
        [
            pltpu.VMEM((side + 2 * margin, width), F32),
            pltpu.VMEM((taps, side + 2 * margin, width), BF),
        ],
        flops=2 * bases * side * width * taps * (block + taps - 1),
        data=2 * bases * side * width,
        name="filter",
    )(toeplitz, *pieces, *halos)
    return kernel_call(
        functools.partial(finish_body, visits, bands),
        jax.ShapeDtypeStruct((visit_count, side, width), BF),
        [SMEM] * 2 + [VMEM] * (2 + visits),
        [pltpu.VMEM((visit_count, side, width), BF)],
        flops=20 * visit_count * side * width,
        data=4 * visit_count * side * width,
        name="finish",
    )(basis_choice, coef_table, filtered, plane, *own)


def solution(mesh):
    return jax.shard_map(
        on_device,
        mesh=mesh,
        in_specs=(
            P(("group", "visit", "band"), "sky", None, None),
            P(("group", "visit", "band"), "sky", None),
            P(("group", "visit", "band"), "sky"),
            P(),
            P(("group", "visit", "band"), "sky"),
            P("group", "sky", None),
            P(),
            P(("group", "visit", "band"), "sky"),
            P(),
        ),
        out_specs=P(("group", "visit", "band"), "sky", None),
        check_vma=False,
    )
```

time: 323 us -> 56.5 us (0.17)
  local copies, waits for them, and re-layouts: 196 us -> 6.45 us
  waiting for transfers between devices: 54.8 us -> 10.9 us
  matrix products: 31.6 us -> 0 us
  Pallas kernels: 0 us -> 19.4 us
  between operations: 13.5 us -> 0.14 us
  other arithmetic: 10 us -> 0.02 us
  starting transfers between devices: 15 us -> 19.3 us
    gather x2 -> x0, local copies, waits for them, and re-layouts: 147 us -> none  [banded_filter(): bands = jnp.take(kernels, jnp.clip(offsets, 0, kernel_side - 1), axis=2)]
    dot_general x14 -> x0, matrix products: 31.6 us -> none  [the longest x8 19.5 us: one_tile(): jnp.einsum('adx,bdxc->bac', shifted, bands, preferred_element_type=jnp.fl...]
    all_to_all x2 -> x0, waiting for transfers between devices: 30.5 us -> none  [the longest x1 30.5 us: on_device(): lax.all_to_all(outgoing.reshape(visit_count, patches, capacity * tile_are...]
    while x257 -> x0, local copies, waits for them, and re-layouts: 29.8 us -> none
    all_gather x1 -> x0, waiting for transfers between devices: 20.7 us -> none  [on_device(): lax.all_gather(banded_filter(padded, own_kernels, tile_side, tile_cols),...]
    pallas_call x0 -> x6, Pallas kernels: none -> 19.4 us  [the longest x1 6.72 us: on_device(): kernel_call(functools.partial(filter_body, visits, margin), jax.ShapeDtyp...]
    ppermute x2 -> x12, starting transfers between devices: 3.28 us -> 19.3 us  [the longest x7 15.3 us: on_device(): arrived.append(lax.ppermute(parcels[n], ('sky', 'visit'), pairs))]
    all_to_all x2 -> x0, starting transfers between devices: 11.6 us -> none  [the longest x1 6.35 us: on_device(): lax.all_to_all(labels.reshape(visit_count, patches, capacity), 'sky', spl...]
  transfers between devices with their start and end apart: 8 -> 12, of which waited for: 3 -> 4; matrix products, arithmetic and copies ran while one was open for 52% -> 3% of each run, Pallas kernels for 0% -> 16%
where the time goes in v1:
time: 56.5 us; the launch traced here: 56.2 us
  Pallas kernels  19.4 us (34%)
  starting transfers between devices  19.3 us (34%)
  waiting for transfers between devices  10.9 us (19%)
  local copies, waits for them, and re-layouts  6.45 us (11%)
    ppermute x7, starting transfers between devices, on_device(): arrived.append(lax.ppermute(parcels[n], ('sky', 'visit'), pairs))  15.3 us
    pallas_call x1, Pallas kernels, on_device(): kernel_call(functools.partial(filter_body, visits, margin), jax.ShapeDtyp...  6.72 us
    unnamed x36, local copies, waits for them, and re-layouts  5.75 us
    ppermute x2, waiting for transfers between devices, on_device(): halos.append(lax.ppermute(edge, ('sky', 'visit'), top + bottom))  5.34 us
    ppermute x7, waiting for transfers between devices, on_device(): arrived.append(lax.ppermute(parcels[n], ('sky', 'visit'), pairs))  3.62 us
    pallas_call x1, Pallas kernels, land_tiles(): kernel_call(functools.partial(land_body, visits, bands, visit_count, cap)...  2.9 us
    pallas_call x1, Pallas kernels, on_device(): kernel_call(functools.partial(finish_body, visits, bands), jax.ShapeDtype...  2.86 us
    pallas_call x1, Pallas kernels, warp_tiles(): kernel_call(functools.partial(warp_body, patches, visits, cap), [parcel]...  2.57 us
  transfers between devices with their start and end apart: 12, of which 4 were waited for; matrix products, arithmetic and copies ran while one was open for 3% of the time, Pallas kernels for 16%

profile of v1, /device:TPU:0, one launch (start us, length us, event | category | flops | bytes accessed | tf_op | source)
XLA Modules:
  0.0 56.2 jit_solution(7827932667082265398)
XLA Ops:
  0.0 1.4 %copy.20.offsets = s32[2,8,2]{2,1,0:T(8,128)} copy(s32[2,8,2]{1,2,0:T(2,128)} %param.10) | data formatting | bytes 256 | tf_op args[1]
  1.4 0.0 copy-done.11
  1.4 0.7 %copy.21.table = f32[16,2]{1,0:T(8,128)} copy(f32[16,2]{0,1:T(2,128)S(1)} %copy-done.11) | data formatting | bytes 256 | tf_op args[3]
  2.1 2.6 %warp.1 = (bf16[328,128]{1,0:T(8,128)(2,1)}, bf16[328,128]{1,0:T(8,128)(2,1)}, bf16[328,128]{1,0:T(8,128)(2,1)}, bf16[328,128]{1,0:T(8,128)(2,1)}, bf16[328,128]...) custom-call(s32[2,8]{1,0:T(2,128)} %routes.1, ...), custom_call_target="tpu_custom_call" | custom-call | flops 134217728 | bytes 1048576 | tf_op jit(solution)/shard_map/warp/pallas_call | solution.py:95
  4.6 4.1 %collective-permute-start = (bf16[328,128]{1,0:T(8,128)(2,1)}, bf16[328,128]{1,0:T(8,128)(2,1)S(1)}, u32[]{:S(2)}, u32[]{:S(2)}) collective-permute-start(bf16[328,128]{1,0:T(8,128)(2,1)} %get-tuple-element.23), channel_id=1, source_target_pairs={{0,8},{2,10},{4,12},{6,14},{8,0},{10,2},{12,4},{14,6},{1,9},{3,11}... | collective-permute-start | bytes 251912 | tf_op jit(solution)/shard_map/ppermute | solution.py:325
  8.7 1.3 %collective-permute-start.1 = (bf16[328,128]{1,0:T(8,128)(2,1)}, bf16[328,128]{1,0:T(8,128)(2,1)S(1)}, u32[]{:S(2)}, u32[]{:S(2)}) collective-permute-start(bf16[328,128]{1,0:T(8,128)(2,1)} %get-tuple-element.24), channel_id=1, source_target_pairs={{0,10},{2,8},{4,14},{6,12},{8,2},{10,0},{12,6},{14,4},{1,11},{3,9}... | collective-permute-start | bytes 251912 | tf_op jit(solution)/shard_map/ppermute | solution.py:325
  10.0 1.6 %collective-permute-start.2 = (bf16[328,128]{1,0:T(8,128)(2,1)}, bf16[328,128]{1,0:T(8,128)(2,1)S(1)}, u32[]{:S(2)}, u32[]{:S(2)}) collective-permute-start(bf16[328,128]{1,0:T(8,128)(2,1)} %get-tuple-element.25), channel_id=1, source_target_pairs={{0,4},{2,6},{4,8},{6,10},{8,12},{10,14},{12,0},{14,2},{1,5},{3,7},... | collective-permute-start | bytes 251912 | tf_op jit(solution)/shard_map/ppermute | solution.py:325
  11.5 1.5 %collective-permute-start.3 = (bf16[328,128]{1,0:T(8,128)(2,1)}, bf16[328,128]{1,0:T(8,128)(2,1)S(1)}, u32[]{:S(2)}, u32[]{:S(2)}) collective-permute-start(bf16[328,128]{1,0:T(8,128)(2,1)} %get-tuple-element.26), channel_id=1, source_target_pairs={{0,6},{2,4},{4,10},{6,8},{8,14},{10,12},{12,2},{14,0},{1,7},{3,5},... | collective-permute-start | bytes 251912 | tf_op jit(solution)/shard_map/ppermute | solution.py:325
  13.1 2.2 %collective-permute-start.4 = (bf16[328,128]{1,0:T(8,128)(2,1)}, bf16[328,128]{1,0:T(8,128)(2,1)S(1)}, u32[]{:S(2)}, u32[]{:S(2)}) collective-permute-start(bf16[328,128]{1,0:T(8,128)(2,1)} %get-tuple-element.27), channel_id=1, source_target_pairs={{0,12},{2,14},{4,0},{6,2},{8,4},{10,6},{12,8},{14,10},{1,13},{3,15... | collective-permute-start | bytes 251912 | tf_op jit(solution)/shard_map/ppermute | solution.py:325
  15.3 0.0 copy-done.9
  15.3 0.1 copy.18
  15.5 0.0 collective-permute-done.refs_1_
  15.5 4.2 %collective-permute-start.5 = (bf16[328,128]{1,0:T(8,128)(2,1)}, bf16[328,128]{1,0:T(8,128)(2,1)S(1)}, u32[]{:S(2)}, u32[]{:S(2)}) collective-permute-start(bf16[328,128]{1,0:T(8,128)(2,1)} %get-tuple-element.28), channel_id=1, source_target_pairs={{0,14},{2,12},{4,2},{6,0},{8,6},{10,4},{12,10},{14,8},{1,15},{3,13... | collective-permute-start | bytes 251912 | tf_op jit(solution)/shard_map/ppermute | solution.py:325
  19.7 2.5 %collective-permute-done.1.refs_2_ = bf16[328,128]{1,0:T(8,128)(2,1)S(1)} collective-permute-done((bf16[328,128]{1,0:T(8,128)(2,1)}, bf16[328,128]{1,0:T(8,128)(2,1)S(1)}, u32[]{:S(2)}, u32[]{:S(2)}) %collective-permute-start.1) | collective-permute-done | bytes 84000 | tf_op jit(solution)/shard_map/ppermute | solution.py:325
  22.2 0.5 collective-permute-start.6
  22.7 0.0 copy-done.2
  22.7 0.1 copy-done.3
  22.8 0.7 %reshape.8.taps = f32[4,17,128]{2,1,0:T(8,128)} reshape(f32[4,34,64]{2,1,0:T(8,128)S(1)} %copy.19) | data formatting | bytes 69632 | tf_op jit(solution)/shard_map/reshape | solution.py:141
  23.5 2.2 %tables.1 = (f32[128,1024]{1,0:T(8,128)}, bf16[128,2176]{1,0:T(8,128)(2,1)}) custom-call(s32[8,8,32]{2,1,0:T(8,128)} %listed.1, f32[4,17,128]{2,1,0:T(8,128)} %reshape.8.taps), custom_call_target="tpu_custom_call" | custom-call | flops 67108864 | bytes 524288 | tf_op jit(solution)/shard_map/tables/pallas_call | solution.py:142
  25.7 0.0 collective-permute-done.2.refs_3_
  25.7 0.0 collective-permute-done.3.refs_4_
  25.7 0.0 copy-start.5
  25.7 0.0 collective-permute-done.4.refs_5_
  25.8 0.0 copy-start.6
  25.8 0.0 collective-permute-done.5.refs_6_
  25.8 0.0 copy-start.7
  25.8 1.1 %collective-permute-done.6.refs_7_ = bf16[328,128]{1,0:T(8,128)(2,1)S(1)} collective-permute-done((bf16[328,128]{1,0:T(8,128)(2,1)}, bf16[328,128]{1,0:T(8,128)(2,1)S(1)}, u32[]{:S(2)}, u32[]{:S(2)}) %collective-permute-start.6) | collective-permute-done | bytes 84000 | tf_op jit(solution)/shard_map/ppermute | solution.py:325
  26.9 0.0 copy-done.4
  26.9 0.6 %copy-done.8 = bf16[328,128]{1,0:T(8,128)(2,1)} copy-done((bf16[328,128]{1,0:T(8,128)(2,1)}, bf16[328,128]{1,0:T(8,128)(2,1)S(1)}, u32[]{:S(2)}) %copy-start.8) | copy-done | bytes 83992
  27.5 2.9 %land.1 = (bf16[2,64,1024]{2,1,0:T(8,128)(2,1)}, bf16[2,64,1024]{2,1,0:T(8,128)(2,1)}, bf16[3,64,1024]{2,1,0:T(8,128)(2,1)}) custom-call(f32[128,1024]{1,0:T(8,128)} %get-tuple-element.21.plane, bf16[328,128]{1,0:T(8,128)(2,1)} %get-tuple-element.22.refs_0_, bf16[328,128]{1,0:T(8,128)(2,1)} %copy-done.2, bf16[328,128]{1,0:T(8,128)(2,1)} %copy-done.3, ...), custom_call_target="tpu_custom_call" | custom-call | flops 2621440 | bytes 1048576 | tf_op jit(solution)/shard_map/land/pallas_call | solution.py:198
  30.4 0.0 collective-permute-start.7
  30.4 1.9 %collective-permute-done.7.refs_1_ = bf16[3,64,1024]{2,1,0:T(8,128)(2,1)S(1)} collective-permute-done((bf16[3,64,1024]{2,1,0:T(8,128)(2,1)}, bf16[3,64,1024]{2,1,0:T(8,128)(2,1)S(1)}, u32[]{:S(2)}, u32[]{:S(2)}) %collective-permute-start.7) | collective-permute-done | bytes 393248 | tf_op jit(solution)/shard_map/ppermute | solution.py:330
  32.3 0.8 %copy-done = bf16[3,64,1024]{2,1,0:T(8,128)(2,1)} copy-done((bf16[3,64,1024]{2,1,0:T(8,128)(2,1)}, bf16[3,64,1024]{2,1,0:T(8,128)(2,1)S(1)}, u32[]{:S(2)}) %copy-start) | copy-done | bytes 393240
  33.1 2.1 %coadd.1 = (bf16[64,1024]{1,0:T(8,128)(2,1)}, bf16[16,1024]{1,0:T(8,128)(2,1)}) custom-call(f32[128,1024]{1,0:T(8,128)} %get-tuple-element.21.plane, bf16[3,64,1024]{2,1,0:T(8,128)(2,1)} %get-tuple-element.30.refs_0_, bf16[3,64,1024]{2,1,0:T(8,128)(2,1)} %copy-done), custom_call_target="tpu_custom_call" | custom-call | flops 524288 | bytes 524288 | tf_op jit(solution)/shard_map/coadd/pallas_call | solution.py:333
  35.2 0.6 %collective-permute-start.8 = (bf16[64,1024]{1,0:T(8,128)(2,1)}, bf16[64,1024]{1,0:T(8,128)(2,1)S(1)}, u32[]{:S(2)}, u32[]{:S(2)}) collective-permute-start(bf16[64,1024]{1,0:T(8,128)(2,1)} %get-tuple-element.31.refs_0_), channel_id=1, source_target_pairs={{0,2},{2,0},{1,3},{3,1},{4,6},{6,4},{5,7},{7,5},{8,10},{10,8},{9,1... | collective-permute-start | bytes 393224 | tf_op jit(solution)/shard_map/ppermute | solution.py:345
  35.8 1.4 %collective-permute-start.11 = (bf16[2,64,1024]{2,1,0:T(8,128)(2,1)S(1)}, bf16[2,64,1024]{2,1,0:T(8,128)(2,1)S(1)}, u32[]{:S(2)}, u32[]{:S(2)}) collective-permute-start(bf16[2,64,1024]{2,1,0:T(8,128)(2,1)S(1)} %copy-done.12), channel_id=1, source_target_pairs={{0,2},{2,0},{1,3},{3,1},{4,6},{6,4},{5,7},{7,5},{8,10},{10,8},{9,1... | collective-permute-start | bytes 786440 | tf_op jit(solution)/shard_map/ppermute | solution.py:354
  37.3 0.7 %collective-permute-start.10 = (bf16[16,1024]{1,0:T(8,128)(2,1)}, bf16[16,1024]{1,0:T(8,128)(2,1)S(1)}, u32[]{:S(2)}, u32[]{:S(2)}) collective-permute-start(bf16[16,1024]{1,0:T(8,128)(2,1)} %get-tuple-element.32), channel_id=1, source_target_pairs={{4,2},{8,6},{12,10},{2,4},{6,8},{10,12},{5,3},{9,7},{13,11},{3,5},... | collective-permute-start | bytes 98312 | tf_op jit(solution)/shard_map/ppermute | solution.py:352
  37.9 1.3 %collective-permute-start.9 = (bf16[16,1024]{1,0:T(8,128)(2,1)}, bf16[16,1024]{1,0:T(8,128)(2,1)S(1)}, u32[]{:S(2)}, u32[]{:S(2)}) collective-permute-start(bf16[16,1024]{1,0:T(8,128)(2,1)} %get-tuple-element.32), channel_id=1, source_target_pairs={{4,0},{8,4},{12,8},{2,6},{6,10},{10,14},{5,1},{9,5},{13,9},{3,7},{... | collective-permute-start | bytes 98312 | tf_op jit(solution)/shard_map/ppermute | solution.py:352
  39.2 0.7 %copy.22.coefs = f32[16,4]{1,0:T(8,128)} copy(f32[16,4]{0,1:T(4,128)S(1)} %copy-done.10) | data formatting | bytes 512 | tf_op args[8]
  39.9 0.0 collective-permute-done.10.refs_3_
  39.9 5.3 %collective-permute-done.9.refs_2_ = bf16[16,1024]{1,0:T(8,128)(2,1)S(1)} collective-permute-done((bf16[16,1024]{1,0:T(8,128)(2,1)}, bf16[16,1024]{1,0:T(8,128)(2,1)S(1)}, u32[]{:S(2)}, u32[]{:S(2)}) %collective-permute-start.9) | collective-permute-done | bytes 32800 | tf_op jit(solution)/shard_map/ppermute | solution.py:352
  45.2 0.0 collective-permute-done.8.refs_1_
  45.3 0.6 %copy-done.15 = bf16[16,1024]{1,0:T(8,128)(2,1)} copy-done((bf16[16,1024]{1,0:T(8,128)(2,1)}, bf16[16,1024]{1,0:T(8,128)(2,1)S(1)}, u32[]{:S(2)}) %copy-start.15) | copy-done | bytes 32792
  45.8 0.1 copy-done.13
  45.9 6.7 %filter.1.filtered = bf16[4,128,1024]{2,1,0:T(8,128)(2,1)} custom-call(bf16[128,2176]{1,0:T(8,128)(2,1)} %get-tuple-element.20.bands, bf16[64,1024]{1,0:T(8,128)(2,1)} %get-tuple-element.31.refs_0_, bf16[64,1024]{1,0:T(8,128)(2,1)} %copy-done.13, bf16[16,1024]{1,0:T(8,128)(2,1)} %copy-done.15, bf16[16,1024]{1,0:T(8,128)(2,1)} %copy-done.14), custom_call_target="tpu_custom_call" | custom-call | flops 2214592512 | bytes 1048576 | tf_op jit(solution)/shard_map/filter/pallas_call | solution.py:358
  52.6 0.0 collective-permute-done.11.refs_1_
  52.6 0.7 %copy-done.1 = bf16[2,64,1024]{2,1,0:T(8,128)(2,1)} copy-done((bf16[2,64,1024]{2,1,0:T(8,128)(2,1)}, bf16[2,64,1024]{2,1,0:T(8,128)(2,1)S(1)}, u32[]{:S(2)}) %copy-start.1) | copy-done | bytes 262168
  53.3 2.9 %finish.1 = bf16[2,128,1024]{2,1,0:T(8,128)(2,1)} custom-call(s32[2,8]{1,0:T(2,128)} %choice.1, f32[16,4]{1,0:T(8,128)} %copy.22.coefs, bf16[4,128,1024]{2,1,0:T(8,128)(2,1)} %filter.1.filtered, f32[128,1024]{1,0:T(8,128)} %get-tuple-element.21.plane, bf16[2,64,1024]{2,1,0:T(8,128)(2,1)} %get-tuple-element.33.refs_0_, bf16[2,64,1024]{2,1,0:T(8,128)(2,1)} %copy-done.1), custom_call_target="tpu_custom_call" | custom-call | flops 5242880 | bytes 1048576 | tf_op jit(solution)/shard_map/finish/pallas_call | solution.py:370
  (21 shorter events, 0.1 us)
Async XLA Ops:
  0.0 1.4 %copy-start.11 = (f32[16,2]{0,1:T(2,128)S(1)}, f32[16,2]{0,1:T(2,128)}, u32[]{:S(2)}) copy-start(f32[16,2]{0,1:T(2,128)} %param.12) | copy-start | bytes 388
  2.0 13.3 %copy-start.9 = (bf16[4,33,33]{2,0,1:T(4,128)(2,1)S(1)}, bf16[4,33,33]{2,0,1:T(4,128)(2,1)}, u32[]{:S(2)}) copy-start(bf16[4,33,33]{2,0,1:T(4,128)(2,1)} %param.15) | copy-start | bytes 26140
  4.6 10.8 %collective-permute-start = (bf16[328,128]{1,0:T(8,128)(2,1)}, bf16[328,128]{1,0:T(8,128)(2,1)S(1)}, u32[]{:S(2)}, u32[]{:S(2)}) collective-permute-start(bf16[328,128]{1,0:T(8,128)(2,1)} %get-tuple-element.23), channel_id=1, source_target_pairs={{0,8},{2,10},{4,12},{6,14},{8,0},{10,2},{12,4},{14,6},{1,9},{3,11}... | collective-permute-start | bytes 251912 | tf_op jit(solution)/shard_map/ppermute | solution.py:325
  8.7 13.5 %collective-permute-start.1 = (bf16[328,128]{1,0:T(8,128)(2,1)}, bf16[328,128]{1,0:T(8,128)(2,1)S(1)}, u32[]{:S(2)}, u32[]{:S(2)}) collective-permute-start(bf16[328,128]{1,0:T(8,128)(2,1)} %get-tuple-element.24), channel_id=1, source_target_pairs={{0,10},{2,8},{4,14},{6,12},{8,2},{10,0},{12,6},{14,4},{1,11},{3,9}... | collective-permute-start | bytes 251912 | tf_op jit(solution)/shard_map/ppermute | solution.py:325
  10.0 15.8 %collective-permute-start.2 = (bf16[328,128]{1,0:T(8,128)(2,1)}, bf16[328,128]{1,0:T(8,128)(2,1)S(1)}, u32[]{:S(2)}, u32[]{:S(2)}) collective-permute-start(bf16[328,128]{1,0:T(8,128)(2,1)} %get-tuple-element.25), channel_id=1, source_target_pairs={{0,4},{2,6},{4,8},{6,10},{8,12},{10,14},{12,0},{14,2},{1,5},{3,7},... | collective-permute-start | bytes 251912 | tf_op jit(solution)/shard_map/ppermute | solution.py:325
  11.5 14.2 %collective-permute-start.3 = (bf16[328,128]{1,0:T(8,128)(2,1)}, bf16[328,128]{1,0:T(8,128)(2,1)S(1)}, u32[]{:S(2)}, u32[]{:S(2)}) collective-permute-start(bf16[328,128]{1,0:T(8,128)(2,1)} %get-tuple-element.26), channel_id=1, source_target_pairs={{0,6},{2,4},{4,10},{6,8},{8,14},{10,12},{12,2},{14,0},{1,7},{3,5},... | collective-permute-start | bytes 251912 | tf_op jit(solution)/shard_map/ppermute | solution.py:325
  13.1 12.7 %collective-permute-start.4 = (bf16[328,128]{1,0:T(8,128)(2,1)}, bf16[328,128]{1,0:T(8,128)(2,1)S(1)}, u32[]{:S(2)}, u32[]{:S(2)}) collective-permute-start(bf16[328,128]{1,0:T(8,128)(2,1)} %get-tuple-element.27), channel_id=1, source_target_pairs={{0,12},{2,14},{4,0},{6,2},{8,4},{10,6},{12,8},{14,10},{1,13},{3,15... | collective-permute-start | bytes 251912 | tf_op jit(solution)/shard_map/ppermute | solution.py:325
  15.5 7.2 %copy-start.2 = (bf16[328,128]{1,0:T(8,128)(2,1)}, bf16[328,128]{1,0:T(8,128)(2,1)S(1)}, u32[]{:S(2)}) copy-start(bf16[328,128]{1,0:T(8,128)(2,1)S(1)} %collective-permute-done.refs_1_) | copy-start | bytes 251908
  15.5 10.3 %collective-permute-start.5 = (bf16[328,128]{1,0:T(8,128)(2,1)}, bf16[328,128]{1,0:T(8,128)(2,1)S(1)}, u32[]{:S(2)}, u32[]{:S(2)}) collective-permute-start(bf16[328,128]{1,0:T(8,128)(2,1)} %get-tuple-element.28), channel_id=1, source_target_pairs={{0,14},{2,12},{4,2},{6,0},{8,6},{10,4},{12,10},{14,8},{1,15},{3,13... | collective-permute-start | bytes 251912 | tf_op jit(solution)/shard_map/ppermute | solution.py:325
  22.2 0.6 %copy-start.3 = (bf16[328,128]{1,0:T(8,128)(2,1)}, bf16[328,128]{1,0:T(8,128)(2,1)S(1)}, u32[]{:S(2)}) copy-start(bf16[328,128]{1,0:T(8,128)(2,1)S(1)} %collective-permute-done.1.refs_2_) | copy-start | bytes 251908
  22.2 4.7 %collective-permute-start.6 = (bf16[328,128]{1,0:T(8,128)(2,1)}, bf16[328,128]{1,0:T(8,128)(2,1)S(1)}, u32[]{:S(2)}, u32[]{:S(2)}) collective-permute-start(bf16[328,128]{1,0:T(8,128)(2,1)} %get-tuple-element.29), channel_id=1, source_target_pairs={{0,2},{2,0},{4,6},{6,4},{8,10},{10,8},{12,14},{14,12},{1,3},{3,1},... | collective-permute-start | bytes 251912 | tf_op jit(solution)/shard_map/ppermute | solution.py:325
  25.7 1.1 %copy-start.4 = (bf16[328,128]{1,0:T(8,128)(2,1)}, bf16[328,128]{1,0:T(8,128)(2,1)S(1)}, u32[]{:S(2)}) copy-start(bf16[328,128]{1,0:T(8,128)(2,1)S(1)} %collective-permute-done.2.refs_3_) | copy-start | bytes 251908
  25.7 1.1 %copy-start.5 = (bf16[328,128]{1,0:T(8,128)(2,1)}, bf16[328,128]{1,0:T(8,128)(2,1)S(1)}, u32[]{:S(2)}) copy-start(bf16[328,128]{1,0:T(8,128)(2,1)S(1)} %collective-permute-done.3.refs_4_) | copy-start | bytes 251908
  25.8 1.1 %copy-start.6 = (bf16[328,128]{1,0:T(8,128)(2,1)}, bf16[328,128]{1,0:T(8,128)(2,1)S(1)}, u32[]{:S(2)}) copy-start(bf16[328,128]{1,0:T(8,128)(2,1)S(1)} %collective-permute-done.4.refs_5_) | copy-start | bytes 251908
  25.8 1.1 %copy-start.7 = (bf16[328,128]{1,0:T(8,128)(2,1)}, bf16[328,128]{1,0:T(8,128)(2,1)S(1)}, u32[]{:S(2)}) copy-start(bf16[328,128]{1,0:T(8,128)(2,1)S(1)} %collective-permute-done.5.refs_6_) | copy-start | bytes 251908
  26.9 0.6 %copy-start.8 = (bf16[328,128]{1,0:T(8,128)(2,1)}, bf16[328,128]{1,0:T(8,128)(2,1)S(1)}, u32[]{:S(2)}) copy-start(bf16[328,128]{1,0:T(8,128)(2,1)S(1)} %collective-permute-done.6.refs_7_) | copy-start | bytes 251908
  30.4 5.4 %copy-start.12 = (bf16[2,64,1024]{2,1,0:T(8,128)(2,1)S(1)}, bf16[2,64,1024]{2,1,0:T(8,128)(2,1)}, u32[]{:S(2)}) copy-start(bf16[2,64,1024]{2,1,0:T(8,128)(2,1)} %get-tuple-element.34) | copy-start | bytes 786436
  30.4 1.9 %collective-permute-start.7 = (bf16[3,64,1024]{2,1,0:T(8,128)(2,1)}, bf16[3,64,1024]{2,1,0:T(8,128)(2,1)S(1)}, u32[]{:S(2)}, u32[]{:S(2)}) collective-permute-start(bf16[3,64,1024]{2,1,0:T(8,128)(2,1)} %get-tuple-element.30.refs_0_), channel_id=1, source_target_pairs={{0,1},{1,0},{2,3},{3,2},{4,5},{5,4},{6,7},{7,6},{8,9},{9,8},{10,11... | collective-permute-start | bytes 1179656 | tf_op jit(solution)/shard_map/ppermute | solution.py:330
  32.3 0.8 %copy-start = (bf16[3,64,1024]{2,1,0:T(8,128)(2,1)}, bf16[3,64,1024]{2,1,0:T(8,128)(2,1)S(1)}, u32[]{:S(2)}) copy-start(bf16[3,64,1024]{2,1,0:T(8,128)(2,1)S(1)} %collective-permute-done.7.refs_1_) | copy-start | bytes 1179652
  35.2 4.0 %copy-start.10 = (f32[16,4]{0,1:T(4,128)S(1)}, f32[16,4]{0,1:T(4,128)}, u32[]{:S(2)}) copy-start(f32[16,4]{0,1:T(4,128)} %param.17) | copy-start | bytes 772
  35.2 10.0 %collective-permute-start.8 = (bf16[64,1024]{1,0:T(8,128)(2,1)}, bf16[64,1024]{1,0:T(8,128)(2,1)S(1)}, u32[]{:S(2)}, u32[]{:S(2)}) collective-permute-start(bf16[64,1024]{1,0:T(8,128)(2,1)} %get-tuple-element.31.refs_0_), channel_id=1, source_target_pairs={{0,2},{2,0},{1,3},{3,1},{4,6},{6,4},{5,7},{7,5},{8,10},{10,8},{9,1... | collective-permute-start | bytes 393224 | tf_op jit(solution)/shard_map/ppermute | solution.py:345
  35.8 16.8 %collective-permute-start.11 = (bf16[2,64,1024]{2,1,0:T(8,128)(2,1)S(1)}, bf16[2,64,1024]{2,1,0:T(8,128)(2,1)S(1)}, u32[]{:S(2)}, u32[]{:S(2)}) collective-permute-start(bf16[2,64,1024]{2,1,0:T(8,128)(2,1)S(1)} %copy-done.12), channel_id=1, source_target_pairs={{0,2},{2,0},{1,3},{3,1},{4,6},{6,4},{5,7},{7,5},{8,10},{10,8},{9,1... | collective-permute-start | bytes 786440 | tf_op jit(solution)/shard_map/ppermute | solution.py:354
  37.3 2.6 %collective-permute-start.10 = (bf16[16,1024]{1,0:T(8,128)(2,1)}, bf16[16,1024]{1,0:T(8,128)(2,1)S(1)}, u32[]{:S(2)}, u32[]{:S(2)}) collective-permute-start(bf16[16,1024]{1,0:T(8,128)(2,1)} %get-tuple-element.32), channel_id=1, source_target_pairs={{4,2},{8,6},{12,10},{2,4},{6,8},{10,12},{5,3},{9,7},{13,11},{3,5},... | collective-permute-start | bytes 98312 | tf_op jit(solution)/shard_map/ppermute | solution.py:352
  37.9 7.3 %collective-permute-start.9 = (bf16[16,1024]{1,0:T(8,128)(2,1)}, bf16[16,1024]{1,0:T(8,128)(2,1)S(1)}, u32[]{:S(2)}, u32[]{:S(2)}) collective-permute-start(bf16[16,1024]{1,0:T(8,128)(2,1)} %get-tuple-element.32), channel_id=1, source_target_pairs={{4,0},{8,4},{12,8},{2,6},{6,10},{10,14},{5,1},{9,5},{13,9},{3,7},{... | collective-permute-start | bytes 98312 | tf_op jit(solution)/shard_map/ppermute | solution.py:352
  39.9 5.4 %copy-start.14 = (bf16[16,1024]{1,0:T(8,128)(2,1)}, bf16[16,1024]{1,0:T(8,128)(2,1)S(1)}, u32[]{:S(2)}) copy-start(bf16[16,1024]{1,0:T(8,128)(2,1)S(1)} %collective-permute-done.10.refs_3_) | copy-start | bytes 98308
  45.2 0.6 %copy-start.15 = (bf16[16,1024]{1,0:T(8,128)(2,1)}, bf16[16,1024]{1,0:T(8,128)(2,1)S(1)}, u32[]{:S(2)}) copy-start(bf16[16,1024]{1,0:T(8,128)(2,1)S(1)} %collective-permute-done.9.refs_2_) | copy-start | bytes 98308
  45.2 0.7 %copy-start.13 = (bf16[64,1024]{1,0:T(8,128)(2,1)}, bf16[64,1024]{1,0:T(8,128)(2,1)S(1)}, u32[]{:S(2)}) copy-start(bf16[64,1024]{1,0:T(8,128)(2,1)S(1)} %collective-permute-done.8.refs_1_) | copy-start | bytes 393220
  52.6 0.7 %copy-start.1 = (bf16[2,64,1024]{2,1,0:T(8,128)(2,1)}, bf16[2,64,1024]{2,1,0:T(8,128)(2,1)S(1)}, u32[]{:S(2)}) copy-start(bf16[2,64,1024]{2,1,0:T(8,128)(2,1)S(1)} %collective-permute-done.11.refs_1_) | copy-start | bytes 786436
